TPU v7x, 256 devices: a whole 4x4x8 slice. The times are simulated.
256 devices in a mesh: east: 32 (over z, y_hi, core), north: 8 (over x, y_lo).
Axes of the slice: x: 4, y: 4 (y_hi: 2, y_lo: 2; y = y_hi * 2 + y_lo), z: 8, core: 2. Of those that a mesh axis runs over, the one named last changes fastest.
Arguments:
- features: bfloat16 [96, 256, 128, 8], P(None, 'east', 'north'), may hold values from -6 to 6
- brick_active: int32 [32, 16, 1], P('east', 'north'), may hold values 0 or 1
- voxel_occupancy: int32 [256, 128, 8], P('east', 'north'), may hold values 0 or 1
- first_weights: bfloat16 [27, 96, 96], replicated, may hold values from -0.125 to 0.125
- second_weights: bfloat16 [27, 96, 96], replicated, may hold values from -0.125 to 0.125
- head: bfloat16 [13, 96], replicated, may hold values from -0.625 to 0.625
- teacher: bfloat16 [13, 256, 128, 8], P(None, 'east', 'north'), may hold values from -6 to 6
Outputs:
- grad_features: bfloat16 [96, 256, 128, 8], P(None, 'east', 'north')
- grad_first: float32 [27, 96, 96], replicated
- grad_second: float32 [27, 96, 96], replicated
All inputs are finite; a program needn't handle non-finite values. No bound on the sum of `brick_active` or of `voxel_occupancy` on one device may be relied on, other than what follows from the above.
Results may differ from a plain program's by a relative error of at most 0.0058.
Values may be sent and summed in bfloat16 or wider, within the bound.
A program may use at most 128 MiB of HBM per device.

v0:
```python
import math
import jax
import jax.numpy as jnp
from jax import lax
from jax.sharding import PartitionSpec as P


def padded(block, sides, width):
    for axis, dim in sides:
        count = lax.axis_size(axis)
        forward = [(i, i + 1) for i in range(count - 1)]
        backward = [(target, source) for source, target in forward]
        low = lax.ppermute(
            lax.slice_in_dim(block, block.shape[dim] - width, None, axis=dim), axis, forward
        )
        high = lax.ppermute(lax.slice_in_dim(block, 0, width, axis=dim), axis, backward)
        block = jnp.concatenate([low, block, high], axis=dim)
    return block


def offset_of(k):
    return (k // 9 - 1, k // 3 % 3 - 1, k % 3 - 1)


def silu_slope(value):
    sig = jax.nn.sigmoid(value)
    return sig * (1.0 + value * (1.0 - sig))


def stacked(field, sign):
    channels, east, north, plane = field.shape
    wider = padded(field, (("east", 1), ("north", 2)), 1)
    flat = wider.reshape(channels, east + 2, (north + 2) * plane)
    flat = jnp.pad(flat, ((0, 0), (0, 0), (1, 1)))
    pieces = []
    for k in range(27):
        de, dn, du = offset_of(k)
        first = 1 + sign * de
        start = (1 + sign * dn) * plane + sign * du + 1
        pieces.append(flat[:, first : first + east, start : start + north * plane])
    return jnp.stack(pieces, 0).reshape(27 * channels, east * north * plane)


def arrange(part, outputs, channels):
    return part.reshape(outputs, 27, channels).transpose(1, 0, 2)


def per_device(
    features, brick_active, voxel_occupancy, first_weights, second_weights, head, teacher
):
    channels = features.shape[0]
    shape = features.shape[1:]
    east, north, upward = shape
    plane = upward + 2
    wide_shape = (channels, east, north, plane)
    flags = jnp.repeat(brick_active, east // brick_active.shape[0], 0)
    flags = jnp.repeat(flags, north // brick_active.shape[1], 1)
    flags = jnp.repeat(flags, upward // brick_active.shape[2], 2)
    mask = jnp.pad((flags * voxel_occupancy).astype(jnp.float32), ((0, 0), (0, 0), (1, 1)))
    flat_mask = mask.reshape(1, -1)
    wide_features = jnp.pad(features, ((0, 0), (0, 0), (0, 0), (1, 1)))
    a0 = jnp.where(mask[None] > 0, wide_features, jnp.zeros_like(wide_features))
    forward_one = first_weights.transpose(1, 0, 2).reshape(channels, 27 * channels)
    forward_two = second_weights.transpose(1, 0, 2).reshape(channels, 27 * channels)
    backward_one = first_weights.transpose(2, 0, 1).reshape(channels, 27 * channels)
    backward_two = second_weights.transpose(2, 0, 1).reshape(channels, 27 * channels)
    stack_zero = stacked(a0, 1)
    p1 = flat_mask * jnp.dot(forward_one, stack_zero, preferred_element_type=jnp.float32)
    a1 = jax.nn.silu(p1).astype(jnp.bfloat16)
    stack_one = stacked(a1.reshape(wide_shape), 1)
    p2 = flat_mask * jnp.dot(forward_two, stack_one, preferred_element_type=jnp.float32)
    a2 = jax.nn.silu(p2).astype(jnp.bfloat16)
    logits = jnp.dot(head, a2, preferred_element_type=jnp.float32)
    wide_teacher = jnp.pad(teacher, ((0, 0), (0, 0), (0, 0), (1, 1))).reshape(teacher.shape[0], -1)
    g_logits = flat_mask * (logits - wide_teacher.astype(jnp.float32))
    g_a2 = jnp.dot(head.astype(jnp.float32).T, g_logits, precision=lax.Precision.HIGHEST)
    g_p2 = (flat_mask * g_a2 * silu_slope(p2)).astype(jnp.bfloat16)
    total_voxels = lax.axis_size("east") * lax.axis_size("north") * east * north * upward
    scale = 1.0 / math.sqrt(total_voxels)
    contract = (((1,), (1,)), ((), ()))
    second_part = lax.dot_general(g_p2, stack_one, contract, preferred_element_type=jnp.float32)
    second_part = arrange(second_part, channels, channels)
    g_a1 = jnp.dot(
        backward_two, stacked(g_p2.reshape(wide_shape), -1), preferred_element_type=jnp.float32
    )
    g_p1 = (flat_mask * g_a1 * silu_slope(p1)).astype(jnp.bfloat16)
    first_part = lax.dot_general(g_p1, stack_zero, contract, preferred_element_type=jnp.float32)
    first_part = arrange(first_part, channels, channels)
    wide_grad = flat_mask * jnp.dot(
        backward_one, stacked(g_p1.reshape(wide_shape), -1), preferred_element_type=jnp.float32
    )
    grad_features = wide_grad.astype(jnp.bfloat16).reshape(wide_shape)[:, :, :, 1 : plane - 1]
    first_part, second_part = lax.psum((first_part, second_part), ("east", "north"))
    return (grad_features, first_part * scale, second_part * scale)


def solution(mesh):
    in_specs = (
        P(None, "east", "north", None),
        P("east", "north", None),
        P("east", "north", None),
        P(),
        P(),
        P(),
        P(None, "east", "north", None),
    )
    out_specs = (P(None, "east", "north", None), P(), P())
    return jax.shard_map(
        per_device, mesh=mesh, in_specs=in_specs, out_specs=out_specs, check_vma=False
    )
```

profile of v0, /device:TPU:8, one launch (start us, length us, event | category | flops | bytes accessed | tf_op | source)
XLA Modules:
  0.0 724.4 jit_solution(11437631143420705263)
XLA Ops:
  11.6 3.0 collective-permute-start
  15.6 4.1 collective-permute-start.3
  19.7 2.7 collective-permute-start.2
  24.3 2.2 copy.105
  26.7 2.2 copy.108
  32.0 2.6 pad_slice_fusion.6
  55.8 14.9 %copy.104 = bf16[27,96,8,160]{3,2,1,0:T(8,128)(2,1)} copy(bf16[27,96,8,160]{1,3,2,0:T(8,128)(2,1)} %constant_dynamic-update-slice_fusion) | data formatting | bytes 13271040 | tf_op jit(solution)/shard_map/stack | solution.py:41
  70.7 17.5 %reshape.185 = bf16[2592,1280]{1,0:T(8,128)(2,1)} reshape(bf16[27,96,8,160]{3,2,1,0:T(8,128)(2,1)} %copy.104) | data formatting | bytes 13271040 | tf_op jit(solution)/shard_map/reshape | solution.py:41
  88.2 5.2 multiply_convert_fusion.1
  96.1 4.9 collective-permute-start.4
  102.7 1.8 copy.116
  109.8 1.8 copy.119
  118.9 1.8 copy.124
  120.8 1.9 copy.125
  124.5 1.8 copy.127
  131.8 1.8 copy.131
  133.6 1.8 copy.132
  175.5 1.9 collective-permute-start.7
  177.5 4.8 collective-permute-start.6
  186.9 2.6 pad_slice_fusion
  210.8 14.9 %copy.107 = bf16[27,96,8,160]{3,2,1,0:T(8,128)(2,1)} copy(bf16[27,96,8,160]{1,3,2,0:T(8,128)(2,1)} %constant_dynamic-update-slice_fusion.30) | data formatting | bytes 13271040 | tf_op jit(solution)/shard_map/stack | solution.py:41
  225.6 17.5 %reshape.189 = bf16[2592,1280]{1,0:T(8,128)(2,1)} reshape(bf16[27,96,8,160]{3,2,1,0:T(8,128)(2,1)} %copy.107) | data formatting | bytes 13271040 | tf_op jit(solution)/shard_map/reshape | solution.py:41
  243.2 4.3 fusion.3
  251.6 5.8 collective-permute-start.8
  267.9 1.8 copy.147
  271.6 1.8 copy.149
  275.2 1.9 copy.151
  277.1 1.8 copy.152
  278.9 1.8 copy.153
  280.8 1.8 copy.154
  282.6 1.8 copy.155
  288.1 1.9 copy.158
  331.8 1.9 collective-permute-start.11
  333.7 4.8 collective-permute-start.10
  362.8 14.9 %copy.112 = bf16[27,96,8,160]{3,2,1,0:T(8,128)(2,1)} copy(bf16[27,96,8,160]{1,3,2,0:T(8,128)(2,1)} %constant_dynamic-update-slice_fusion.60) | data formatting | bytes 13271040 | tf_op jit(solution)/shard_map/stack | solution.py:41
  377.6 17.6 %reshape.193 = bf16[2592,1280]{1,0:T(8,128)(2,1)} reshape(bf16[27,96,8,160]{3,2,1,0:T(8,128)(2,1)} %copy.112) | data formatting | bytes 13271040 | tf_op jit(solution)/shard_map/reshape | solution.py:41
  395.3 4.3 fusion.6
  400.0 6.5 collective-permute-start.12
  406.5 6.5 convolution_bitcast_fusion.1
  414.6 4.9 collective-permute-done.13
  419.5 1.9 collective-permute-start.15
  421.4 5.9 collective-permute-start.14
  427.3 6.4 convolution_bitcast_fusion.2
  456.4 14.9 %copy.114 = bf16[27,96,8,160]{3,2,1,0:T(8,128)(2,1)} copy(bf16[27,96,8,160]{1,3,2,0:T(8,128)(2,1)} %constant_dynamic-update-slice_fusion.90) | data formatting | bytes 13271040 | tf_op jit(solution)/shard_map/stack | solution.py:41
  471.3 17.6 %reshape.197 = bf16[2592,1280]{1,0:T(8,128)(2,1)} reshape(bf16[27,96,8,160]{3,2,1,0:T(8,128)(2,1)} %copy.114) | data formatting | bytes 13271040 | tf_op jit(solution)/shard_map/reshape | solution.py:41
  489.0 4.2 fusion.9
  494.4 219.6 %all-reduce.10.cloned.1.call-done = (f32[27,96,96]{2,1,0:T(8,128)}, f32[27,96,96]{2,1,0:T(8,128)}) async-done(((f32[27,96,96]{2,1,0:T(8,128)}, f32[27,96,96]{2,1,0:T(8,128)}), (f32[27,96,96]{2,1,0:T(8,128)}, f32[27,96,96]{2,1,0:T(8,128)})) %all-reduce.10.cloned.1.call-update) | async-done | bytes 1990672 | tf_op jit(solution)/shard_map/psum | solution.py:93
  713.9 3.4 broadcast_multiply_fusion
  (289 shorter events, 235.4 us)
Async XLA Ops:
  7.2 240.3 %copy-start = (bf16[13,96]{1,0:T(8,128)(2,1)S(1)}, bf16[13,96]{1,0:T(8,128)(2,1)}, u32[]{:S(2)}) copy-start(bf16[13,96]{1,0:T(8,128)(2,1)} %param.12) | copy-start | bytes 7492
  7.2 706.8 %all-reduce.10.cloned.1.call-start = ((), (), s32[]{:S(2)}) async-start(), calls=%async_computation | async-start | bytes 5308416 | tf_op jit(solution)/shard_map/psum | solution.py:93
  10.3 5.3 collective-permute-start.1
  11.6 4.0 collective-permute-start
  15.6 13.2 %collective-permute-start.3 = (bf16[96,10,1,10]{0,3,2,1:T(8,128)(2,1)S(1)}, bf16[96,10,1,10]{0,3,2,1:T(8,128)(2,1)S(1)}, u32[]{:S(2)}, u32[]{:S(2)}) collective-permute-start(bf16[96,10,1,10]{0,3,2,1:T(8,128)(2,1)S(1)} %get-tuple-element.12), channel_id=1, source_target_pairs={{1,0},{2,1},{3,2},{4,3},{5,4},{6,5},{7,6},{9,8},{10,9},{11,10},{12... | collective-permute-start | bytes 57608 | tf_op jit(solution)/shard_map/ppermute | solution.py:16
  19.7 9.2 %collective-permute-start.2 = (bf16[96,10,1,10]{0,3,2,1:T(8,128)(2,1)S(1)}, bf16[96,10,1,10]{0,3,2,1:T(8,128)(2,1)S(1)}, u32[]{:S(2)}, u32[]{:S(2)}) collective-permute-start(bf16[96,10,1,10]{0,3,2,1:T(8,128)(2,1)S(1)} %get-tuple-element.11), channel_id=1, source_target_pairs={{0,1},{1,2},{2,3},{3,4},{4,5},{5,6},{6,7},{8,9},{9,10},{10,11},{11... | collective-permute-start | bytes 57608 | tf_op jit(solution)/shard_map/ppermute | solution.py:13
  96.1 78.5 %collective-permute-start.4 = (bf16[96,1,16,10]{0,3,2,1:T(8,128)(2,1)}, bf16[96,1,16,10]{0,3,2,1:T(8,128)(2,1)}, u32[]{:S(2)}, u32[]{:S(2)}) collective-permute-start(bf16[96,1,16,10]{0,3,2,1:T(8,128)(2,1)} %get-tuple-element.18), channel_id=1, source_target_pairs={{0,8},{8,16},{16,24},{24,32},{32,40},{40,48},{48,56},{56,64},{64,7... | collective-permute-start | bytes 92168 | tf_op jit(solution)/shard_map/ppermute | solution.py:13
  100.9 74.6 %collective-permute-start.5 = (bf16[96,1,16,10]{0,3,2,1:T(8,128)(2,1)}, bf16[96,1,16,10]{0,3,2,1:T(8,128)(2,1)S(1)}, u32[]{:S(2)}, u32[]{:S(2)}) collective-permute-start(bf16[96,1,16,10]{0,3,2,1:T(8,128)(2,1)} %get-tuple-element.17), channel_id=1, source_target_pairs={{8,0},{16,8},{24,16},{32,24},{40,32},{48,40},{56,48},{64,56},{72,6... | collective-permute-start | bytes 92168 | tf_op jit(solution)/shard_map/ppermute | solution.py:16
  175.5 7.5 %collective-permute-start.7 = (bf16[96,10,1,10]{0,3,2,1:T(8,128)(2,1)S(1)}, bf16[96,10,1,10]{0,3,2,1:T(8,128)(2,1)S(1)}, u32[]{:S(2)}, u32[]{:S(2)}) collective-permute-start(bf16[96,10,1,10]{0,3,2,1:T(8,128)(2,1)S(1)} %get-tuple-element.10), channel_id=1, source_target_pairs={{1,0},{2,1},{3,2},{4,3},{5,4},{6,5},{7,6},{9,8},{10,9},{11,10},{12... | collective-permute-start | bytes 57608 | tf_op jit(solution)/shard_map/ppermute | solution.py:16
  177.5 6.5 collective-permute-start.6
  243.2 4.3 copy-start.6
  248.3 0.7 copy-start.2
  251.6 79.2 %collective-permute-start.8 = (bf16[96,1,16,10]{0,3,2,1:T(8,128)(2,1)}, bf16[96,1,16,10]{0,3,2,1:T(8,128)(2,1)}, u32[]{:S(2)}, u32[]{:S(2)}) collective-permute-start(bf16[96,1,16,10]{0,3,2,1:T(8,128)(2,1)} %get-tuple-element.16), channel_id=1, source_target_pairs={{0,8},{8,16},{16,24},{24,32},{32,40},{40,48},{48,56},{56,64},{64,7... | collective-permute-start | bytes 92168 | tf_op jit(solution)/shard_map/ppermute | solution.py:13
  257.5 74.3 %collective-permute-start.9 = (bf16[96,1,16,10]{0,3,2,1:T(8,128)(2,1)}, bf16[96,1,16,10]{0,3,2,1:T(8,128)(2,1)S(1)}, u32[]{:S(2)}, u32[]{:S(2)}) collective-permute-start(bf16[96,1,16,10]{0,3,2,1:T(8,128)(2,1)} %get-tuple-element.15), channel_id=1, source_target_pairs={{8,0},{16,8},{24,16},{32,24},{40,32},{48,40},{56,48},{64,56},{72,6... | collective-permute-start | bytes 92168 | tf_op jit(solution)/shard_map/ppermute | solution.py:16
  331.8 7.5 %collective-permute-start.11 = (bf16[96,10,1,10]{0,3,2,1:T(8,128)(2,1)S(1)}, bf16[96,10,1,10]{0,3,2,1:T(8,128)(2,1)S(1)}, u32[]{:S(2)}, u32[]{:S(2)}) collective-permute-start(bf16[96,10,1,10]{0,3,2,1:T(8,128)(2,1)S(1)} %get-tuple-element.8), channel_id=1, source_target_pairs={{1,0},{2,1},{3,2},{4,3},{5,4},{6,5},{7,6},{9,8},{10,9},{11,10},{12... | collective-permute-start | bytes 57608 | tf_op jit(solution)/shard_map/ppermute | solution.py:16
  333.7 6.5 collective-permute-start.10
  377.6 17.6 %copy-start.4 = (bf16[27,96,96]{2,1,0:T(8,128)(2,1)S(1)}, bf16[27,96,96]{2,1,0:T(8,128)(2,1)}, u32[]{:S(2)}) copy-start(bf16[27,96,96]{2,1,0:T(8,128)(2,1)} %param.11) | copy-start | bytes 1492996
  377.6 17.6 %copy-start.7 = (f32[96,1280]{1,0:T(8,128)S(1)}, f32[96,1280]{1,0:T(8,128)}, u32[]{:S(2)}) copy-start(f32[96,1280]{1,0:T(8,128)} %get-tuple-element.76) | copy-start | bytes 1474564
  395.3 11.2 %copy-start.3 = (bf16[96,1280]{1,0:T(8,128)(2,1)S(1)}, bf16[96,1280]{1,0:T(8,128)(2,1)}, u32[]{:S(2)}) copy-start(bf16[96,1280]{1,0:T(8,128)(2,1)} %copy-done.2) | copy-start | bytes 737284
  400.0 14.5 %collective-permute-start.12 = (bf16[96,1,16,10]{0,3,2,1:T(8,128)(2,1)S(1)}, bf16[96,1,16,10]{0,3,2,1:T(8,128)(2,1)S(1)}, u32[]{:S(2)}, u32[]{:S(2)}) collective-permute-start(bf16[96,1,16,10]{0,3,2,1:T(8,128)(2,1)S(1)} %get-tuple-element.14), channel_id=1, source_target_pairs={{0,8},{8,16},{16,24},{24,32},{32,40},{40,48},{48,56},{56,64},{64,7... | collective-permute-start | bytes 92168 | tf_op jit(solution)/shard_map/ppermute | solution.py:13
  413.0 6.5 collective-permute-start.13
  419.5 14.3 %collective-permute-start.15 = (bf16[96,10,1,10]{0,3,2,1:T(8,128)(2,1)S(1)}, bf16[96,10,1,10]{0,3,2,1:T(8,128)(2,1)S(1)}, u32[]{:S(2)}, u32[]{:S(2)}) collective-permute-start(bf16[96,10,1,10]{0,3,2,1:T(8,128)(2,1)S(1)} %get-tuple-element.6), channel_id=1, source_target_pairs={{1,0},{2,1},{3,2},{4,3},{5,4},{6,5},{7,6},{9,8},{10,9},{11,10},{12... | collective-permute-start | bytes 57608 | tf_op jit(solution)/shard_map/ppermute | solution.py:16
  421.4 12.4 %collective-permute-start.14 = (bf16[96,10,1,10]{0,3,2,1:T(8,128)(2,1)S(1)}, bf16[96,10,1,10]{0,3,2,1:T(8,128)(2,1)S(1)}, u32[]{:S(2)}, u32[]{:S(2)}) collective-permute-start(bf16[96,10,1,10]{0,3,2,1:T(8,128)(2,1)S(1)} %get-tuple-element.5), channel_id=1, source_target_pairs={{0,1},{1,2},{2,3},{3,4},{4,5},{5,6},{6,7},{8,9},{9,10},{10,11},{11... | collective-permute-start | bytes 57608 | tf_op jit(solution)/shard_map/ppermute | solution.py:13
  471.3 17.7 %copy-start.5 = (bf16[27,96,96]{2,1,0:T(8,128)(2,1)S(1)}, bf16[27,96,96]{2,1,0:T(8,128)(2,1)}, u32[]{:S(2)}) copy-start(bf16[27,96,96]{2,1,0:T(8,128)(2,1)} %param.10) | copy-start | bytes 1492996
  471.3 246.1 %copy-start.1 = (bf16[13,96]{1,0:T(8,128)(2,1)S(1)}, bf16[13,96]{1,0:T(8,128)(2,1)}, u32[]{:S(2)}) copy-start(bf16[13,96]{1,0:T(8,128)(2,1)} %param.12) | copy-start | bytes 7492
Sparse Core Ops, SparseCore 0:
  433.9 280.0 all-reduce.9
where the time goes:
time: 738 us; the launch traced here: 724 us
  local copies, waits for them, and re-layouts  391 us (53%)
  waiting for transfers between devices  226 us (31%)
  starting transfers between devices  54.3 us (7%)
  matrix products  31.7 us (4%)
  between operations  14.9 us (2%)
    psum x1, waiting for transfers between devices, per_device(): lax.psum((first_part, second_part), ('east', 'north'))  220 us
    unnamed x180, local copies, waits for them, and re-layouts  162 us
    another operation x64, local copies, waits for them, and re-layouts, stacked(): return jnp.stack(pieces, 0).reshape(27 * channels, east * north * plane)  135 us
    reshape x4, local copies, waits for them, and re-layouts, stacked(): return jnp.stack(pieces, 0).reshape(27 * channels, east * north * plane)  70.4 us
    ppermute x8, starting transfers between devices, padded(): lax.ppermute(lax.slice_in_dim(block, block.shape[dim] - width, None, axis...  38.5 us
    ppermute x8, starting transfers between devices, padded(): lax.ppermute(lax.slice_in_dim(block, 0, width, axis=dim), axis, backward)  15.8 us
  transfers between devices with their start and end apart: 17, of which 4 were waited for; matrix products, arithmetic and copies ran while one was open for 31% of the time, Pallas kernels for 0%

commit v1 on v0

--- a/solution.py
+++ b/solution.py
@@ -90,7 +90,7 @@
         backward_one, stacked(g_p1.reshape(wide_shape), -1), preferred_element_type=jnp.float32
     )
     grad_features = wide_grad.astype(jnp.bfloat16).reshape(wide_shape)[:, :, :, 1 : plane - 1]
-    first_part, second_part = lax.psum((first_part, second_part), ("east", "north"))
+    first_part, second_part = lax.psum(lax.psum((first_part, second_part), "east"), "north")
     return (grad_features, first_part * scale, second_part * scale)
 
 

time: 738 us -> 882 us (1.20)
  waiting for transfers between devices: 226 us -> 368 us
    psum x1 -> x2, waiting for transfers between devices: 220 us -> 361 us  [the longest x1 273 us: per_device(): lax.psum((first_part, second_part), 'east')]
  transfers between devices with their start and end apart: 17 -> 18, of which waited for: 4 -> 5; matrix products, arithmetic and copies ran while one was open for 31% -> 26% of each run, Pallas kernels for 0% -> 0%
where the time goes in v1:
time: 882 us; the launch traced here: 866 us
  local copies, waits for them, and re-layouts  391 us (44%)
  waiting for transfers between devices  368 us (42%)
  starting transfers between devices  54.3 us (6%)
  matrix products  31.6 us (4%)
  between operations  15 us (2%)
    psum x1, waiting for transfers between devices, per_device(): lax.psum((first_part, second_part), 'east')  273 us
    unnamed x180, local copies, waits for them, and re-layouts  162 us
    another operation x64, local copies, waits for them, and re-layouts, stacked(): return jnp.stack(pieces, 0).reshape(27 * channels, east * north * plane)  135 us
    psum x1, waiting for transfers between devices, per_device(): lax.psum(lax.psum((first_part, second_part), 'east'), 'north')  88 us
    reshape x4, local copies, waits for them, and re-layouts, stacked(): return jnp.stack(pieces, 0).reshape(27 * channels, east * north * plane)  70.3 us
    ppermute x8, starting transfers between devices, padded(): lax.ppermute(lax.slice_in_dim(block, block.shape[dim] - width, None, axis...  38.5 us
  transfers between devices with their start and end apart: 18, of which 5 were waited for; matrix products, arithmetic and copies ran while one was open for 26% of the time, Pallas kernels for 0%

profile of v1, /device:TPU:8, one launch (start us, length us, event | category | flops | bytes accessed | tf_op | source)
XLA Modules:
  0.0 866.0 jit_solution(14470583954235568587)
XLA Ops:
  11.6 3.0 collective-permute-start
  15.6 4.1 collective-permute-start.3
  19.7 2.7 collective-permute-start.2
  24.3 2.2 copy.105
  26.7 2.2 copy.108
  31.9 2.6 pad_slice_fusion.6
  55.8 14.9 %copy.104 = bf16[27,96,8,160]{3,2,1,0:T(8,128)(2,1)} copy(bf16[27,96,8,160]{1,3,2,0:T(8,128)(2,1)} %constant_dynamic-update-slice_fusion) | data formatting | bytes 13271040 | tf_op jit(solution)/shard_map/stack | solution.py:41
  70.7 17.5 %reshape.185 = bf16[2592,1280]{1,0:T(8,128)(2,1)} reshape(bf16[27,96,8,160]{3,2,1,0:T(8,128)(2,1)} %copy.104) | data formatting | bytes 13271040 | tf_op jit(solution)/shard_map/reshape | solution.py:41
  88.3 5.2 multiply_convert_fusion.1
  96.1 4.8 collective-permute-start.4
  109.8 1.8 copy.119
  119.0 1.8 copy.124
  120.8 1.9 copy.125
  122.7 1.8 copy.126
  124.5 1.9 copy.127
  128.2 1.8 copy.129
  131.9 1.9 copy.131
  133.7 1.8 copy.132
  175.7 1.9 collective-permute-start.7
  177.6 4.8 collective-permute-start.6
  187.1 2.6 pad_slice_fusion
  211.0 14.9 %copy.107 = bf16[27,96,8,160]{3,2,1,0:T(8,128)(2,1)} copy(bf16[27,96,8,160]{1,3,2,0:T(8,128)(2,1)} %constant_dynamic-update-slice_fusion.30) | data formatting | bytes 13271040 | tf_op jit(solution)/shard_map/stack | solution.py:41
  225.9 17.5 %reshape.189 = bf16[2592,1280]{1,0:T(8,128)(2,1)} reshape(bf16[27,96,8,160]{3,2,1,0:T(8,128)(2,1)} %copy.107) | data formatting | bytes 13271040 | tf_op jit(solution)/shard_map/reshape | solution.py:41
  243.4 4.3 fusion.3
  251.8 5.8 collective-permute-start.8
  268.1 1.8 copy.147
  275.4 1.8 copy.151
  280.9 1.8 copy.154
  282.8 1.8 copy.155
  288.3 1.8 copy.158
  290.1 1.8 copy.159
  332.1 1.9 collective-permute-start.11
  334.0 4.8 collective-permute-start.10
  363.1 14.9 %copy.112 = bf16[27,96,8,160]{3,2,1,0:T(8,128)(2,1)} copy(bf16[27,96,8,160]{1,3,2,0:T(8,128)(2,1)} %constant_dynamic-update-slice_fusion.60) | data formatting | bytes 13271040 | tf_op jit(solution)/shard_map/stack | solution.py:41
  378.0 17.6 %reshape.193 = bf16[2592,1280]{1,0:T(8,128)(2,1)} reshape(bf16[27,96,8,160]{3,2,1,0:T(8,128)(2,1)} %copy.112) | data formatting | bytes 13271040 | tf_op jit(solution)/shard_map/reshape | solution.py:41
  395.6 4.3 fusion.6
  400.3 6.5 collective-permute-start.12
  406.8 6.5 convolution_bitcast_fusion.1
  414.9 4.9 collective-permute-done.13
  419.8 1.9 collective-permute-start.15
  421.7 5.9 collective-permute-start.14
  427.6 6.4 convolution_bitcast_fusion.2
  451.1 272.8 %all-reduce.12.cloned.1.call-done = (f32[27,96,96]{2,1,0:T(8,128)}, f32[27,96,96]{2,1,0:T(8,128)}) async-done(((f32[27,96,96]{2,1,0:T(8,128)}, f32[27,96,96]{2,1,0:T(8,128)}), (f32[27,96,96]{2,1,0:T(8,128)}, f32[27,96,96]{2,1,0:T(8,128)})) %all-reduce.12.cloned.1.call-update) | async-done | bytes 1990672 | tf_op jit(solution)/shard_map/psum | solution.py:93
  729.6 14.9 %copy.114 = bf16[27,96,8,160]{3,2,1,0:T(8,128)(2,1)} copy(bf16[27,96,8,160]{1,3,2,0:T(8,128)(2,1)} %constant_dynamic-update-slice_fusion.90) | data formatting | bytes 13271040 | tf_op jit(solution)/shard_map/stack | solution.py:41
  744.5 17.6 %reshape.197 = bf16[2592,1280]{1,0:T(8,128)(2,1)} reshape(bf16[27,96,8,160]{3,2,1,0:T(8,128)(2,1)} %copy.114) | data formatting | bytes 13271040 | tf_op jit(solution)/shard_map/reshape | solution.py:41
  762.1 4.2 fusion.9
  767.5 88.0 %all-reduce.14.cloned.1.call-done = (f32[27,96,96]{2,1,0:T(8,128)}, f32[27,96,96]{2,1,0:T(8,128)}) async-done(((f32[27,96,96]{2,1,0:T(8,128)}, f32[27,96,96]{2,1,0:T(8,128)}), (f32[27,96,96]{2,1,0:T(8,128)}, f32[27,96,96]{2,1,0:T(8,128)})) %all-reduce.14.cloned.1.call-update) | async-done | bytes 1990672 | tf_op jit(solution)/shard_map/psum | solution.py:93
  855.5 3.4 broadcast_multiply_fusion
  (292 shorter events, 237.6 us)
Async XLA Ops:
  7.2 240.5 %copy-start = (bf16[13,96]{1,0:T(8,128)(2,1)S(1)}, bf16[13,96]{1,0:T(8,128)(2,1)}, u32[]{:S(2)}) copy-start(bf16[13,96]{1,0:T(8,128)(2,1)} %param.12) | copy-start | bytes 7492
  7.2 716.7 %all-reduce.12.cloned.1.call-start = ((), (), s32[]{:S(2)}) async-start(), calls=%async_computation | async-start | bytes 5308416 | tf_op jit(solution)/shard_map/psum | solution.py:93
  10.3 5.3 collective-permute-start.1
  11.6 4.0 collective-permute-start
  15.6 13.2 %collective-permute-start.3 = (bf16[96,10,1,10]{0,3,2,1:T(8,128)(2,1)S(1)}, bf16[96,10,1,10]{0,3,2,1:T(8,128)(2,1)S(1)}, u32[]{:S(2)}, u32[]{:S(2)}) collective-permute-start(bf16[96,10,1,10]{0,3,2,1:T(8,128)(2,1)S(1)} %get-tuple-element.14), channel_id=1, source_target_pairs={{1,0},{2,1},{3,2},{4,3},{5,4},{6,5},{7,6},{9,8},{10,9},{11,10},{12... | collective-permute-start | bytes 57608 | tf_op jit(solution)/shard_map/ppermute | solution.py:16
  19.7 9.2 %collective-permute-start.2 = (bf16[96,10,1,10]{0,3,2,1:T(8,128)(2,1)S(1)}, bf16[96,10,1,10]{0,3,2,1:T(8,128)(2,1)S(1)}, u32[]{:S(2)}, u32[]{:S(2)}) collective-permute-start(bf16[96,10,1,10]{0,3,2,1:T(8,128)(2,1)S(1)} %get-tuple-element.13), channel_id=1, source_target_pairs={{0,1},{1,2},{2,3},{3,4},{4,5},{5,6},{6,7},{8,9},{9,10},{10,11},{11... | collective-permute-start | bytes 57608 | tf_op jit(solution)/shard_map/ppermute | solution.py:13
  96.1 78.6 %collective-permute-start.4 = (bf16[96,1,16,10]{0,3,2,1:T(8,128)(2,1)}, bf16[96,1,16,10]{0,3,2,1:T(8,128)(2,1)}, u32[]{:S(2)}, u32[]{:S(2)}) collective-permute-start(bf16[96,1,16,10]{0,3,2,1:T(8,128)(2,1)} %get-tuple-element.20), channel_id=1, source_target_pairs={{0,8},{8,16},{16,24},{24,32},{32,40},{40,48},{48,56},{56,64},{64,7... | collective-permute-start | bytes 92168 | tf_op jit(solution)/shard_map/ppermute | solution.py:13
  100.9 74.7 %collective-permute-start.5 = (bf16[96,1,16,10]{0,3,2,1:T(8,128)(2,1)}, bf16[96,1,16,10]{0,3,2,1:T(8,128)(2,1)S(1)}, u32[]{:S(2)}, u32[]{:S(2)}) collective-permute-start(bf16[96,1,16,10]{0,3,2,1:T(8,128)(2,1)} %get-tuple-element.19), channel_id=1, source_target_pairs={{8,0},{16,8},{24,16},{32,24},{40,32},{48,40},{56,48},{64,56},{72,6... | collective-permute-start | bytes 92168 | tf_op jit(solution)/shard_map/ppermute | solution.py:16
  175.7 7.5 collective-permute-start.7
  177.6 6.5 collective-permute-start.6
  243.4 4.3 copy-start.6
  248.5 0.7 copy-start.2
  251.8 79.2 %collective-permute-start.8 = (bf16[96,1,16,10]{0,3,2,1:T(8,128)(2,1)}, bf16[96,1,16,10]{0,3,2,1:T(8,128)(2,1)}, u32[]{:S(2)}, u32[]{:S(2)}) collective-permute-start(bf16[96,1,16,10]{0,3,2,1:T(8,128)(2,1)} %get-tuple-element.18), channel_id=1, source_target_pairs={{0,8},{8,16},{16,24},{24,32},{32,40},{40,48},{48,56},{56,64},{64,7... | collective-permute-start | bytes 92168 | tf_op jit(solution)/shard_map/ppermute | solution.py:13
  257.7 74.3 %collective-permute-start.9 = (bf16[96,1,16,10]{0,3,2,1:T(8,128)(2,1)}, bf16[96,1,16,10]{0,3,2,1:T(8,128)(2,1)S(1)}, u32[]{:S(2)}, u32[]{:S(2)}) collective-permute-start(bf16[96,1,16,10]{0,3,2,1:T(8,128)(2,1)} %get-tuple-element.17), channel_id=1, source_target_pairs={{8,0},{16,8},{24,16},{32,24},{40,32},{48,40},{56,48},{64,56},{72,6... | collective-permute-start | bytes 92168 | tf_op jit(solution)/shard_map/ppermute | solution.py:16
  332.1 7.5 collective-permute-start.11
  334.0 6.5 collective-permute-start.10
  378.0 17.6 %copy-start.4 = (bf16[27,96,96]{2,1,0:T(8,128)(2,1)S(1)}, bf16[27,96,96]{2,1,0:T(8,128)(2,1)}, u32[]{:S(2)}) copy-start(bf16[27,96,96]{2,1,0:T(8,128)(2,1)} %param.11) | copy-start | bytes 1492996
  378.0 17.6 %copy-start.7 = (f32[96,1280]{1,0:T(8,128)S(1)}, f32[96,1280]{1,0:T(8,128)}, u32[]{:S(2)}) copy-start(f32[96,1280]{1,0:T(8,128)} %get-tuple-element.78) | copy-start | bytes 1474564
  395.6 11.2 %copy-start.3 = (bf16[96,1280]{1,0:T(8,128)(2,1)S(1)}, bf16[96,1280]{1,0:T(8,128)(2,1)}, u32[]{:S(2)}) copy-start(bf16[96,1280]{1,0:T(8,128)(2,1)} %copy-done.2) | copy-start | bytes 737284
  400.3 14.5 %collective-permute-start.12 = (bf16[96,1,16,10]{0,3,2,1:T(8,128)(2,1)S(1)}, bf16[96,1,16,10]{0,3,2,1:T(8,128)(2,1)S(1)}, u32[]{:S(2)}, u32[]{:S(2)}) collective-permute-start(bf16[96,1,16,10]{0,3,2,1:T(8,128)(2,1)S(1)} %get-tuple-element.16), channel_id=1, source_target_pairs={{0,8},{8,16},{16,24},{24,32},{32,40},{40,48},{48,56},{56,64},{64,7... | collective-permute-start | bytes 92168 | tf_op jit(solution)/shard_map/ppermute | solution.py:13
  413.3 6.5 collective-permute-start.13
  419.8 14.4 %collective-permute-start.15 = (bf16[96,10,1,10]{0,3,2,1:T(8,128)(2,1)S(1)}, bf16[96,10,1,10]{0,3,2,1:T(8,128)(2,1)S(1)}, u32[]{:S(2)}, u32[]{:S(2)}) collective-permute-start(bf16[96,10,1,10]{0,3,2,1:T(8,128)(2,1)S(1)} %get-tuple-element.8), channel_id=1, source_target_pairs={{1,0},{2,1},{3,2},{4,3},{5,4},{6,5},{7,6},{9,8},{10,9},{11,10},{12... | collective-permute-start | bytes 57608 | tf_op jit(solution)/shard_map/ppermute | solution.py:16
  421.7 12.4 %collective-permute-start.14 = (bf16[96,10,1,10]{0,3,2,1:T(8,128)(2,1)S(1)}, bf16[96,10,1,10]{0,3,2,1:T(8,128)(2,1)S(1)}, u32[]{:S(2)}, u32[]{:S(2)}) collective-permute-start(bf16[96,10,1,10]{0,3,2,1:T(8,128)(2,1)S(1)} %get-tuple-element.7), channel_id=1, source_target_pairs={{0,1},{1,2},{2,3},{3,4},{4,5},{5,6},{6,7},{8,9},{9,10},{10,11},{11... | collective-permute-start | bytes 57608 | tf_op jit(solution)/shard_map/ppermute | solution.py:13
  434.1 421.4 %all-reduce.14.cloned.1.call-start = ((), (), s32[]{:S(2)}) async-start(), calls=%async_computation.1 | async-start | bytes 5308416 | tf_op jit(solution)/shard_map/psum | solution.py:93
  744.5 17.6 %copy-start.5 = (bf16[27,96,96]{2,1,0:T(8,128)(2,1)S(1)}, bf16[27,96,96]{2,1,0:T(8,128)(2,1)}, u32[]{:S(2)}) copy-start(bf16[27,96,96]{2,1,0:T(8,128)(2,1)} %param.10) | copy-start | bytes 1492996
  744.5 114.4 %copy-start.1 = (bf16[13,96]{1,0:T(8,128)(2,1)S(1)}, bf16[13,96]{1,0:T(8,128)(2,1)}, u32[]{:S(2)}) copy-start(bf16[13,96]{1,0:T(8,128)(2,1)} %param.12) | copy-start | bytes 7492
Sparse Core Ops, SparseCore 0:
  434.2 289.5 all-reduce.11
  726.6 128.8 all-reduce.13
